TPU v7x, 512 devices: a whole 4x8x8 slice. The times are simulated.
512 devices in a mesh: grp: 8 (over y), sp: 64 (over x, z, core).
Axes of the slice: x: 4, y: 8, z: 8, core: 2. Of those that a mesh axis runs over, the one named last changes fastest.
Arguments:
- snapshots: float32 [3, 8192, 24576], P(None, 'grp', 'sp'), may hold values from -12 to 12
- kept_bins: int32 [64], replicated, may hold values from 1 to 255, as said below
- weights: float32 [24576], P('sp'), may hold values from 0.1 to 80
Outputs:
- mode_fields: float32 [2, 64, 4, 3, 24576], P(None, 'grp', None, None, 'sp')
- energies: float32 [64, 4], P('grp')
Inputs may be any that keep to these rules, and one draw needn't show every extreme that they name: `kept_bins`: 64 distinct bins in increasing order; both 1 and 255 are among them.
All inputs are finite; a program needn't handle non-finite values.
Results may differ from a plain program's by a relative error of at most 0.0003.
Values sent between devices are 32-bit elements; how exact they have to be, the bound alone decides.
A program may use at most 64 MiB of HBM per device.

v0:
```python
import math
import jax
import jax.numpy as jnp
from jax import lax
from jax.sharding import PartitionSpec as P

L = 512
HOP = 256
MODES = 4
ITERS = 3
precise = lax.Precision.HIGHEST


def make_table(kept_bins, block_len):
    offsets = jnp.arange(block_len, dtype=jnp.int32)
    phases = kept_bins[:, None] * offsets[None, :] % block_len
    angles = phases.astype(jnp.float32) * (2.0 * math.pi / block_len)
    window = (
        0.5 - 0.5 * jnp.cos(offsets.astype(jnp.float32) * (2.0 * math.pi / block_len))
    ) / math.sqrt(3.0 * block_len / 8.0)
    return jnp.stack([window * jnp.cos(angles), -window * jnp.sin(angles)])


def orthonormalize(w_real, w_imag):
    basis_re = []
    basis_im = []
    lengths = []
    for column in range(w_real.shape[-1]):
        orig_re = w_real[..., column]
        orig_im = w_imag[..., column]
        left_re = orig_re
        left_im = orig_im
        for earlier in range(column):
            prev_re = basis_re[earlier]
            prev_im = basis_im[earlier]
            coef_re = jnp.sum(prev_re * orig_re + prev_im * orig_im, axis=-1, keepdims=True)
            coef_im = jnp.sum(prev_re * orig_im - prev_im * orig_re, axis=-1, keepdims=True)
            left_re = left_re - (coef_re * prev_re - coef_im * prev_im)
            left_im = left_im - (coef_re * prev_im + coef_im * prev_re)
        length = jnp.sqrt(jnp.sum(left_re * left_re + left_im * left_im, axis=-1) + 1e-06)
        basis_re.append(left_re / length[..., None])
        basis_im.append(left_im / length[..., None])
        lengths.append(length)
    return (jnp.stack(basis_re, -1), jnp.stack(basis_im, -1), jnp.stack(lengths, -1))


def apply_gram(gram_re, gram_im, v_real, v_imag):
    pattern = "fbd,fdm->fbm"
    out_re = jnp.einsum(pattern, gram_re, v_real, precision=precise) - jnp.einsum(
        pattern, gram_im, v_imag, precision=precise
    )
    out_im = jnp.einsum(pattern, gram_re, v_imag, precision=precise) + jnp.einsum(
        pattern, gram_im, v_real, precision=precise
    )
    return (out_re, out_im)


def subspace(apply_fn, freq_count, block_count, mode_count):
    identity_cols = jnp.eye(block_count, mode_count, dtype=jnp.float32)
    v_real = jnp.broadcast_to(identity_cols, (freq_count, block_count, mode_count))
    v_imag = jnp.zeros((freq_count, block_count, mode_count), jnp.float32)
    lengths = jnp.zeros((freq_count, mode_count), jnp.float32)
    for sweep_step in range(ITERS):
        w_real, w_imag = apply_fn(v_real, v_imag)
        v_real, v_imag, lengths = orthonormalize(w_real, w_imag)
    return (v_real, v_imag, lengths)


def local_gram(x_real, x_imag, point_wts, norm_factor):
    y_real = x_real * point_wts
    y_imag = x_imag * point_wts
    pattern = "bfcp,dfcp->fbd"
    g_re = (
        jnp.einsum(pattern, y_real, x_real, precision=precise)
        + jnp.einsum(pattern, y_imag, x_imag, precision=precise)
    ) * norm_factor
    g_im = (
        jnp.einsum(pattern, y_real, x_imag, precision=precise)
        - jnp.einsum(pattern, y_imag, x_real, precision=precise)
    ) * norm_factor
    return (g_re, g_im)


def form_modes(x_real, x_imag, v_real, v_imag, lengths, block_count):
    pattern = "bfcp,fbm->fmcp"
    m_re = jnp.einsum(pattern, x_real, v_real, precision=precise) - jnp.einsum(
        pattern, x_imag, v_imag, precision=precise
    )
    m_im = jnp.einsum(pattern, x_real, v_imag, precision=precise) + jnp.einsum(
        pattern, x_imag, v_real, precision=precise
    )
    factor = (1.0 / jnp.sqrt(block_count * lengths))[:, :, None, None]
    return jnp.stack([m_re * factor, m_im * factor])


def total_gram(gram_parts):
    return lax.psum((gram_parts[0], gram_parts[1]), "sp")


def shards(snapshots, kept_bins, weights):
    dft_table = make_table(kept_bins, L)
    local_points = weights.shape[0]
    block_local = snapshots.shape[1] // HOP
    block_count = block_local * lax.axis_size("grp")
    norm_factor = 1.0 / (3.0 * local_points * lax.axis_size("sp"))
    regrouped = lax.all_to_all(snapshots, "grp", split_axis=2, concat_axis=1, tiled=True)
    sub_points = regrouped.shape[2]
    segments = regrouped.reshape(3, block_count, HOP, sub_points)
    following = jnp.roll(segments, -1, axis=1)
    blocks = jnp.concatenate([segments, following], axis=2)
    spectra = jnp.einsum("kft,cbtp->bkfcp", dft_table, blocks, precision=precise)
    x_real = spectra[:, 0]
    x_imag = spectra[:, 1]
    sub_wts = lax.dynamic_slice_in_dim(weights, lax.axis_index("grp") * sub_points, sub_points)
    g_re, g_im = local_gram(x_real, x_imag, sub_wts, norm_factor)
    g_re, g_im = (
        lax.psum_scatter(g_re, "grp", scatter_dimension=0, tiled=True),
        lax.psum_scatter(g_im, "grp", scatter_dimension=0, tiled=True),
    )
    g_re, g_im = total_gram((g_re, g_im))
    freq_count = g_re.shape[0]

    def apply_fn(v_real, v_imag):
        return apply_gram(g_re, g_im, v_real, v_imag)

    v_real, v_imag, lengths = subspace(apply_fn, freq_count, block_count, MODES)
    all_re, all_im, all_len = (
        lax.all_gather(v_real, "grp", axis=0, tiled=True),
        lax.all_gather(v_imag, "grp", axis=0, tiled=True),
        lax.all_gather(lengths, "grp", axis=0, tiled=True),
    )
    mode_fields = form_modes(x_real, x_imag, all_re, all_im, all_len, block_count)
    mode_fields = lax.all_to_all(mode_fields, "grp", split_axis=1, concat_axis=4, tiled=True)
    return (mode_fields, lengths)


def solution(mesh):
    in_specs = (P(None, "grp", "sp"), P(), P("sp"))
    out_specs = (P(None, "grp", None, None, "sp"), P("grp", None))
    return jax.shard_map(shards, mesh=mesh, in_specs=in_specs, out_specs=out_specs, check_vma=False)
```

profile of v0, /device:TPU:2, one launch (start us, length us, event | category | flops | bytes accessed | tf_op | source)
XLA Modules:
  0.0 621.5 jit_solution(10956544655818458053)
XLA Ops:
  7.2 7.4 %copy.333 = f32[3,1024,384]{1,0,2:T(4,128)} copy(f32[3,1024,384]{2,1,0:T(8,128)} %param.3) | data formatting | bytes 9437184 | tf_op args[0]
  14.6 7.2 %all-to-all-start = ((f32[3,1024,384]{1,0,2:T(4,128)}), f32[3,1024,384]{1,0,2:T(4,128)}, u32[]{:S(2)}, u32[]{:S(2)}) async-start(f32[3,1024,384]{1,0,2:T(4,128)} %copy.333), calls=%async_computation | async-start | bytes 12582912 | tf_op jit(solution)/shard_map/all_to_all | solution.py:106
  23.3 140.1 %all-to-all-done = f32[3,1024,384]{1,0,2:T(4,128)} async-done(((f32[3,1024,384]{1,0,2:T(4,128)}), f32[3,1024,384]{1,0,2:T(4,128)}, u32[]{:S(2)}, u32[]{:S(2)}) %all-to-all-start) | async-done | bytes 4718624 | tf_op jit(solution)/shard_map/all_to_all | solution.py:106
  163.3 5.5 copy.334
  168.8 4.9 copy.335
  173.7 6.5 %reshape.1735 = f32[3,32,256,48]{2,1,3,0:T(8,128)} reshape(f32[3,8,1024,48]{2,1,3,0:T(8,128)} %copy.335) | data formatting | bytes 9437184 | tf_op jit(solution)/shard_map/reshape | solution.py:108
  180.2 5.1 copy.338
  185.7 7.6 %fusion.5 = f32[32,2,64,3,48]{2,4,1,0,3:T(8,128)S(1)} fusion(f32[3,1,256,48]{2,3,1,0:T(8,128)S(1)} %slice.115, f32[3,31,256,48]{2,3,1,0:T(8,128)S(1)} %slice.114, f32[3,32,256,48]{2,3,1,0:T(8,128)S(1)} %copy.338, f32[1,64,512]{2,1,0:T(8,128)S(1)} %get-tuple-element.104, f32[1,64,512]{2,1,0:T(8,128)S(1)} %get-tuple-element.103), kind=kOutput, calls=%fused_computation.8 | convolution fusion | flops 3628662784 | bytes 12058624 | tf_op jit(solution)/shard_map/kft,cbtp->bkfcp/dot_general | solution.py:111
  193.4 1.9 slice_bitcast_fusion
  195.2 2.6 broadcast_multiply_fusion.1
  197.9 2.8 copy.343
  200.7 3.7 copy.340
  204.4 2.9 copy.341
  207.4 3.7 copy.342
  211.1 5.8 convolution_bitcast_fusion
  217.0 4.8 fusion.9
  222.3 6.8 %convolution_bitcast_fusion.2 = f32[64,32,32]{2,1,0:T(8,128)S(1)} fusion(f32[32,64,3,48]{3,0,2,1:T(8,128)} %copy.342, f32[32,64,3,48]{3,0,2,1:T(8,128)} %copy.343), kind=kOutput, calls=%fused_computation.11 | convolution fusion | flops 113246208 | bytes 2621440 | tf_op jit(solution)/shard_map/bfcp,dfcp->fbd/dot_general | solution.py:75
  229.1 4.8 fusion.7
  234.0 28.4 %reduce-scatter.5.cloned.1.call-done = f32[8,32,32]{2,1,0:T(8,128)} async-done(((f32[64,32,32]{2,1,0:T(8,128)}), f32[8,32,32]{2,1,0:T(8,128)}) %reduce-scatter.5.cloned.1.call-update) | async-done | bytes 32784 | tf_op jit(solution)/shard_map/reduce_scatter | solution.py:118
  262.4 43.0 %reduce-scatter.3.cloned.1.call-done = f32[8,32,32]{2,1,0:T(8,128)} async-done(((f32[64,32,32]{2,1,0:T(8,128)}), f32[8,32,32]{2,1,0:T(8,128)}) %reduce-scatter.3.cloned.1.call-update) | async-done | bytes 32784 | tf_op jit(solution)/shard_map/reduce_scatter | solution.py:117
  305.4 188.0 %all-reduce.3.cloned.1.call-done = (f32[8,32,32]{2,1,0:T(8,128)}, f32[8,32,32]{2,1,0:T(8,128)}) async-done(((f32[8,32,32]{2,1,0:T(8,128)}, f32[8,32,32]{2,1,0:T(8,128)}), (f32[8,32,32]{2,1,0:T(8,128)}, f32[8,32,32]{2,1,0:T(8,128)})) %all-reduce.3.cloned.1.call-update) | async-done | bytes 65552 | tf_op jit(solution)/shard_map/psum | solution.py:97
  513.2 23.7 %all-gather = f32[8,8,4]{1,2,0:T(4,128)S(1)} all-gather(f32[1,8,4]{1,2,0:T(4,128)S(1)} %fusion.200), channel_id=1, replica_groups=mesh['grp'=8,'sp'=64] {'grp'}, dimensions={0}, use_global_device_ids=true | all-gather | bytes 1152 | tf_op jit(solution)/shard_map/all_gather | solution.py:130
  537.0 24.6 %all_gather.10 = f32[64,32,4]{1,2,0:T(4,128)S(1)} all-gather(f32[8,32,4]{1,2,0:T(4,128)S(1)} %copy.370), channel_id=1, replica_groups=mesh['grp'=8,'sp'=64] {'grp'}, dimensions={0}, use_global_device_ids=true | all-gather | bytes 36864 | tf_op jit(solution)/shard_map/all_gather | solution.py:129
  561.6 24.7 %all_gather.9 = f32[64,32,4]{1,2,0:T(4,128)S(1)} all-gather(f32[8,32,4]{1,2,0:T(4,128)S(1)} %copy.368), channel_id=1, replica_groups=mesh['grp'=8,'sp'=64] {'grp'}, dimensions={0}, use_global_device_ids=true | all-gather | bytes 36864 | tf_op jit(solution)/shard_map/all_gather | solution.py:128
  586.3 1.9 fusion.20
  588.2 1.9 fusion.22
  590.2 1.9 fusion.11
  592.1 1.9 fusion.13
  594.3 1.6 reshape.1749
  595.8 3.9 all-to-all-start.1
  600.3 10.2 %all-to-all-done.1 = f32[8,1,9216]{2,1,0:T(1,128)S(1)} async-done(((f32[8,1,9216]{2,1,0:T(1,128)}), f32[8,1,9216]{2,1,0:T(1,128)S(1)}, u32[]{:S(2)}, u32[]{:S(2)}) %all-to-all-start.1) | async-done | bytes 294944 | tf_op jit(solution)/shard_map/all_to_all | solution.py:133
  611.1 1.3 reduce
  (96 shorter events, 25.8 us)
Async XLA Ops:
  14.6 8.1 %copy-start.4 = (s32[64]{0:T(128)S(1)}, s32[64]{0:T(128)}, u32[]{:S(2)}) copy-start(s32[64]{0:T(128)} %param.4) | copy-start | bytes 772
  14.6 148.8 %all-to-all-start = ((f32[3,1024,384]{1,0,2:T(4,128)}), f32[3,1024,384]{1,0,2:T(4,128)}, u32[]{:S(2)}, u32[]{:S(2)}) async-start(f32[3,1024,384]{1,0,2:T(4,128)} %copy.333), calls=%async_computation | async-start | bytes 12582912 | tf_op jit(solution)/shard_map/all_to_all | solution.py:106
  21.8 240.6 %reduce-scatter.5.cloned.1.call-start = ((), (), s32[]{:S(2)}) async-start(), calls=%async_computation.5 | async-start | bytes 1179648 | tf_op jit(solution)/shard_map/reduce_scatter | solution.py:118
  211.1 5.9 copy-start
  211.1 5.9 copy-start.2
  221.8 83.6 %reduce-scatter.3.cloned.1.call-start = ((), (), s32[]{:S(2)}) async-start(), calls=%async_computation.4 | async-start | bytes 1179648 | tf_op jit(solution)/shard_map/reduce_scatter | solution.py:117
  222.3 6.8 %copy-start.3 = (f32[32,64,3,48]{3,0,2,1:T(8,128)S(1)}, f32[32,64,3,48]{3,0,2,1:T(8,128)}, u32[]{:S(2)}) copy-start(f32[32,64,3,48]{3,0,2,1:T(8,128)} %copy.340) | copy-start | bytes 3538948
  233.9 259.5 %all-reduce.3.cloned.1.call-start = ((), (), s32[]{:S(2)}) async-start(), calls=%async_computation.6 | async-start | bytes 524288 | tf_op jit(solution)/shard_map/psum | solution.py:97
  586.3 3.8 copy-start.1
  595.8 14.7 %all-to-all-start.1 = ((f32[8,1,9216]{2,1,0:T(1,128)}), f32[8,1,9216]{2,1,0:T(1,128)S(1)}, u32[]{:S(2)}, u32[]{:S(2)}) async-start(f32[8,1,9216]{2,1,0:T(1,128)} %reshape.1749), calls=%async_computation.3 | async-start | bytes 589824 | tf_op jit(solution)/shard_map/all_to_all | solution.py:133
Sparse Core Ops, SparseCore 0:
  221.9 40.4 reduce-scatter.4
  265.2 40.1 reduce-scatter.2
  308.9 184.4 all-reduce.2
where the time goes:
time: 628 us; the launch traced here: 622 us
  waiting for transfers between devices  410 us (65%)
  blocking collectives  73 us (12%)
  matrix products  52.3 us (8%)
  local copies, waits for them, and re-layouts  50.2 us (8%)
  between operations  14.3 us (2%)
  starting transfers between devices  11.7 us (2%)
  other arithmetic  10.3 us (2%)
    psum x1, waiting for transfers between devices, total_gram(): return lax.psum((gram_parts[0], gram_parts[1]), 'sp')  188 us
    all_to_all x1, waiting for transfers between devices, shards(): lax.all_to_all(snapshots, 'grp', split_axis=2, concat_axis=1, tiled=True)  140 us
    reduce_scatter x1, waiting for transfers between devices, shards(): lax.psum_scatter(g_re, 'grp', scatter_dimension=0, tiled=True)  43 us
    reduce_scatter x1, waiting for transfers between devices, shards(): lax.psum_scatter(g_im, 'grp', scatter_dimension=0, tiled=True)  28.4 us
    all_gather x1, blocking collectives, shards(): lax.all_gather(v_real, 'grp', axis=0, tiled=True)  24.7 us
    all_gather x1, blocking collectives, shards(): lax.all_gather(v_imag, 'grp', axis=0, tiled=True)  24.6 us
    all_gather x1, blocking collectives, shards(): lax.all_gather(lengths, 'grp', axis=0, tiled=True)  23.7 us
  transfers between devices with their start and end apart: 5, of which 5 were waited for; matrix products, arithmetic and copies ran while one was open for 2% of the time, Pallas kernels for 0%

commit v1 on v0

--- a/solution.py
+++ b/solution.py
@@ -126,7 +126,9 @@
     v_real, v_imag, lengths = subspace(apply_fn, freq_count, block_count, MODES)
     all_re, all_im, all_len = (
         lax.all_gather(v_real, "grp", axis=0, tiled=True),
-        lax.all_gather(v_imag, "grp", axis=0, tiled=True),
+        jnp.concatenate(
+            lax.all_to_all(jnp.stack([v_imag] * lax.axis_size("grp")), "grp", 0, 0), axis=0
+        ),
         lax.all_gather(lengths, "grp", axis=0, tiled=True),
     )
     mode_fields = form_modes(x_real, x_imag, all_re, all_im, all_len, block_count)

time: 628 us -> 623 us (level)
  blocking collectives: 73 us -> 51.8 us
    all_gather x1 -> x0, blocking collectives: 24.6 us -> none  [shards(): lax.all_gather(v_imag, 'grp', axis=0, tiled=True)]
  transfers between devices with their start and end apart: 5 -> 6, of which waited for: 5 -> 6; matrix products, arithmetic and copies ran while one was open for 2% -> 3% of each run, Pallas kernels for 0% -> 0%
where the time goes in v1:
time: 623 us; the launch traced here: 616 us
  waiting for transfers between devices  414 us (66%)
  matrix products  54.3 us (9%)
  local copies, waits for them, and re-layouts  53.3 us (9%)
  blocking collectives  51.8 us (8%)
  starting transfers between devices  15.7 us (3%)
  between operations  14.5 us (2%)
  other arithmetic  12.3 us (2%)
    psum x1, waiting for transfers between devices, total_gram(): return lax.psum((gram_parts[0], gram_parts[1]), 'sp')  188 us
    all_to_all x1, waiting for transfers between devices, shards(): lax.all_to_all(snapshots, 'grp', split_axis=2, concat_axis=1, tiled=True)  140 us
    reduce_scatter x1, waiting for transfers between devices, shards(): lax.psum_scatter(g_re, 'grp', scatter_dimension=0, tiled=True)  43 us
    reduce_scatter x1, waiting for transfers between devices, shards(): lax.psum_scatter(g_im, 'grp', scatter_dimension=0, tiled=True)  28.4 us
    all_gather x1, blocking collectives, shards(): lax.all_gather(v_real, 'grp', axis=0, tiled=True)  26.6 us
    all_gather x1, blocking collectives, shards(): lax.all_gather(lengths, 'grp', axis=0, tiled=True)  25.1 us
  transfers between devices with their start and end apart: 6, of which 6 were waited for; matrix products, arithmetic and copies ran while one was open for 3% of the time, Pallas kernels for 0%

profile of v1, /device:TPU:2, one launch (start us, length us, event | category | flops | bytes accessed | tf_op | source)
XLA Modules:
  0.0 616.0 jit_solution(14817924703017297112)
XLA Ops:
  7.2 7.4 %copy.333 = f32[3,1024,384]{1,0,2:T(4,128)} copy(f32[3,1024,384]{2,1,0:T(8,128)} %param.3) | data formatting | bytes 9437184 | tf_op args[0]
  14.6 7.2 %all-to-all-start = ((f32[3,1024,384]{1,0,2:T(4,128)}), f32[3,1024,384]{1,0,2:T(4,128)}, u32[]{:S(2)}, u32[]{:S(2)}) async-start(f32[3,1024,384]{1,0,2:T(4,128)} %copy.333), calls=%async_computation | async-start | bytes 12582912 | tf_op jit(solution)/shard_map/all_to_all | solution.py:106
  23.3 140.1 %all-to-all-done = f32[3,1024,384]{1,0,2:T(4,128)} async-done(((f32[3,1024,384]{1,0,2:T(4,128)}), f32[3,1024,384]{1,0,2:T(4,128)}, u32[]{:S(2)}, u32[]{:S(2)}) %all-to-all-start) | async-done | bytes 4718624 | tf_op jit(solution)/shard_map/all_to_all | solution.py:106
  163.3 5.5 copy.334
  168.8 4.9 copy.335
  173.7 6.5 %reshape.1740 = f32[3,32,256,48]{2,1,3,0:T(8,128)} reshape(f32[3,8,1024,48]{2,1,3,0:T(8,128)} %copy.335) | data formatting | bytes 9437184 | tf_op jit(solution)/shard_map/reshape | solution.py:108
  180.2 5.1 copy.338
  185.7 7.6 %fusion.5 = f32[32,2,64,3,48]{2,4,1,0,3:T(8,128)S(1)} fusion(f32[3,1,256,48]{2,3,1,0:T(8,128)S(1)} %slice.115, f32[3,31,256,48]{2,3,1,0:T(8,128)S(1)} %slice.114, f32[3,32,256,48]{2,3,1,0:T(8,128)S(1)} %copy.338, f32[1,64,512]{2,1,0:T(8,128)S(1)} %get-tuple-element.104, f32[1,64,512]{2,1,0:T(8,128)S(1)} %get-tuple-element.103), kind=kOutput, calls=%fused_computation.8 | convolution fusion | flops 3628662784 | bytes 12058624 | tf_op jit(solution)/shard_map/kft,cbtp->bkfcp/dot_general | solution.py:111
  193.4 1.9 slice_bitcast_fusion
  195.3 2.7 broadcast_multiply_fusion.1
  198.0 2.8 copy.343
  200.8 3.7 copy.340
  204.6 2.9 copy.341
  207.5 3.7 copy.342
  211.2 5.8 convolution_bitcast_fusion
  217.1 4.8 fusion.9
  222.4 6.8 %convolution_bitcast_fusion.2 = f32[64,32,32]{2,1,0:T(8,128)S(1)} fusion(f32[32,64,3,48]{3,0,2,1:T(8,128)} %copy.342, f32[32,64,3,48]{3,0,2,1:T(8,128)} %copy.343), kind=kOutput, calls=%fused_computation.11 | convolution fusion | flops 113246208 | bytes 2621440 | tf_op jit(solution)/shard_map/bfcp,dfcp->fbd/dot_general | solution.py:75
  229.2 4.8 fusion.7
  234.2 28.4 %reduce-scatter.5.cloned.1.call-done = f32[8,32,32]{2,1,0:T(8,128)} async-done(((f32[64,32,32]{2,1,0:T(8,128)}), f32[8,32,32]{2,1,0:T(8,128)}) %reduce-scatter.5.cloned.1.call-update) | async-done | bytes 32784 | tf_op jit(solution)/shard_map/reduce_scatter | solution.py:118
  262.5 43.0 %reduce-scatter.3.cloned.1.call-done = f32[8,32,32]{2,1,0:T(8,128)} async-done(((f32[64,32,32]{2,1,0:T(8,128)}), f32[8,32,32]{2,1,0:T(8,128)}) %reduce-scatter.3.cloned.1.call-update) | async-done | bytes 32784 | tf_op jit(solution)/shard_map/reduce_scatter | solution.py:117
  305.6 188.1 %all-reduce.3.cloned.1.call-done = (f32[8,32,32]{2,1,0:T(8,128)}, f32[8,32,32]{2,1,0:T(8,128)}) async-done(((f32[8,32,32]{2,1,0:T(8,128)}, f32[8,32,32]{2,1,0:T(8,128)}), (f32[8,32,32]{2,1,0:T(8,128)}, f32[8,32,32]{2,1,0:T(8,128)})) %all-reduce.3.cloned.1.call-update) | async-done | bytes 65552 | tf_op jit(solution)/shard_map/psum | solution.py:97
  513.4 25.1 %all-gather = f32[8,8,4]{1,2,0:T(4,128)} all-gather(f32[1,8,4]{1,2,0:T(4,128)S(1)} %fusion.200), channel_id=1, replica_groups=mesh['grp'=8,'sp'=64] {'grp'}, dimensions={0}, use_global_device_ids=true | all-gather | bytes 1152 | tf_op jit(solution)/shard_map/all_gather | solution.py:132
  538.6 26.6 %all_gather.6 = f32[64,32,4]{1,2,0:T(4,128)} all-gather(f32[8,32,4]{1,2,0:T(4,128)S(1)} %copy.368), channel_id=1, replica_groups=mesh['grp'=8,'sp'=64] {'grp'}, dimensions={0}, use_global_device_ids=true | all-gather | bytes 36864 | tf_op jit(solution)/shard_map/all_gather | solution.py:128
  566.0 4.4 all-to-all-start.1
  570.4 2.8 fusion.20
  573.9 4.6 all-to-all-done.1
  579.0 2.0 reduce
  582.6 3.0 fusion.173
  585.5 1.9 fusion.13
  587.5 1.9 fusion.11
  591.3 3.6 all-to-all-start.2
  595.5 10.1 %all-to-all-done.2 = f32[8,1,9216]{2,1,0:T(1,128)S(1)} async-done(((f32[8,1,9216]{2,1,0:T(1,128)}), f32[8,1,9216]{2,1,0:T(1,128)S(1)}, u32[]{:S(2)}, u32[]{:S(2)}) %all-to-all-start.2) | async-done | bytes 294944 | tf_op jit(solution)/shard_map/all_to_all | solution.py:135
  (125 shorter events, 31.6 us)
Async XLA Ops:
  14.6 8.1 %copy-start.16 = (s32[64]{0:T(128)S(1)}, s32[64]{0:T(128)}, u32[]{:S(2)}) copy-start(s32[64]{0:T(128)} %param.4) | copy-start | bytes 772
  14.6 148.8 %all-to-all-start = ((f32[3,1024,384]{1,0,2:T(4,128)}), f32[3,1024,384]{1,0,2:T(4,128)}, u32[]{:S(2)}, u32[]{:S(2)}) async-start(f32[3,1024,384]{1,0,2:T(4,128)} %copy.333), calls=%async_computation | async-start | bytes 12582912 | tf_op jit(solution)/shard_map/all_to_all | solution.py:106
  21.8 240.7 %reduce-scatter.5.cloned.1.call-start = ((), (), s32[]{:S(2)}) async-start(), calls=%async_computation.6 | async-start | bytes 1179648 | tf_op jit(solution)/shard_map/reduce_scatter | solution.py:118
  211.2 5.9 copy-start
  211.2 5.9 copy-start.2
  222.0 83.6 %reduce-scatter.3.cloned.1.call-start = ((), (), s32[]{:S(2)}) async-start(), calls=%async_computation.5 | async-start | bytes 1179648 | tf_op jit(solution)/shard_map/reduce_scatter | solution.py:117
  222.4 6.8 %copy-start.3 = (f32[32,64,3,48]{3,0,2,1:T(8,128)S(1)}, f32[32,64,3,48]{3,0,2,1:T(8,128)}, u32[]{:S(2)}) copy-start(f32[32,64,3,48]{3,0,2,1:T(8,128)} %copy.340) | copy-start | bytes 3538948
  234.1 259.5 %all-reduce.3.cloned.1.call-start = ((), (), s32[]{:S(2)}) async-start(), calls=%async_computation.7 | async-start | bytes 524288 | tf_op jit(solution)/shard_map/psum | solution.py:97
  511.8 53.4 %copy-start.8 = (f32[8,1]{0,1:T(1,128)}, f32[8,1]{0,1:T(1,128)S(1)}, u32[]{:S(2)}) copy-start(f32[8,1]{0,1:T(1,128)S(1)} %get-tuple-element.95) | copy-start | bytes 100
  512.3 52.9 %copy-start.10 = (f32[8,1]{0,1:T(1,128)}, f32[8,1]{0,1:T(1,128)S(1)}, u32[]{:S(2)}) copy-start(f32[8,1]{0,1:T(1,128)S(1)} %get-tuple-element.97) | copy-start | bytes 100
  512.8 52.4 %copy-start.12 = (f32[8,1]{0,1:T(1,128)}, f32[8,1]{0,1:T(1,128)S(1)}, u32[]{:S(2)}) copy-start(f32[8,1]{0,1:T(1,128)S(1)} %get-tuple-element.99) | copy-start | bytes 100
  513.2 52.0 %copy-start.14 = (f32[8,1]{0,1:T(1,128)}, f32[8,1]{0,1:T(1,128)S(1)}, u32[]{:S(2)}) copy-start(f32[8,1]{0,1:T(1,128)S(1)} %get-tuple-element.101) | copy-start | bytes 100
  566.0 12.5 %all-to-all-start.1 = ((f32[8,1,1024]{2,1,0:T(1,128)}), f32[8,1,1024]{2,1,0:T(1,128)}, u32[]{:S(2)}, u32[]{:S(2)}) async-start(f32[8,1,1024]{2,1,0:T(1,128)} %reshape.1755), calls=%async_computation.3 | async-start | bytes 65536 | tf_op jit(solution)/shard_map/all_to_all | solution.py:130
  570.4 2.8 copy-start.7
  582.5 3.0 copy-start.1
  582.5 3.0 copy-start.5
  582.5 3.0 copy-start.6
  582.5 4.9 copy-start.4
  587.5 7.4 %copy-start.9 = (f32[8,1]{0,1:T(1,128)S(1)}, f32[8,1]{0,1:T(1,128)}, u32[]{:S(2)}) copy-start(f32[8,1]{0,1:T(1,128)} %copy-done.8) | copy-start | bytes 100
  587.5 7.4 %copy-start.11 = (f32[8,1]{0,1:T(1,128)S(1)}, f32[8,1]{0,1:T(1,128)}, u32[]{:S(2)}) copy-start(f32[8,1]{0,1:T(1,128)} %copy-done.10) | copy-start | bytes 100
  587.5 7.4 %copy-start.13 = (f32[8,1]{0,1:T(1,128)S(1)}, f32[8,1]{0,1:T(1,128)}, u32[]{:S(2)}) copy-start(f32[8,1]{0,1:T(1,128)} %copy-done.12) | copy-start | bytes 100
  587.5 7.4 %copy-start.15 = (f32[8,1]{0,1:T(1,128)S(1)}, f32[8,1]{0,1:T(1,128)}, u32[]{:S(2)}) copy-start(f32[8,1]{0,1:T(1,128)} %copy-done.14) | copy-start | bytes 100
  591.3 14.4 %all-to-all-start.2 = ((f32[8,1,9216]{2,1,0:T(1,128)}), f32[8,1,9216]{2,1,0:T(1,128)S(1)}, u32[]{:S(2)}, u32[]{:S(2)}) async-start(f32[8,1,9216]{2,1,0:T(1,128)} %reshape.1757), calls=%async_computation.4 | async-start | bytes 589824 | tf_op jit(solution)/shard_map/all_to_all | solution.py:135
Sparse Core Ops, SparseCore 0:
  222.1 40.4 reduce-scatter.4
  265.4 40.1 reduce-scatter.2
  309.1 184.4 all-reduce.2
